TPU v7x, 32 devices: a whole 2x2x4 slice. The times are simulated.
32 devices in a mesh: grp: 2 (over x), seq: 16 (over z, y, core).
Axes of the slice: x: 2, y: 2, z: 4, core: 2. Of those that a mesh axis runs over, the one named last changes fastest.
Arguments:
- image_qkv: bfloat16 [3, 8, 16, 896, 128], P(None, 'grp', None, 'seq'), parts along dimension 1, may hold values from -16 to 16
- text_kv: bfloat16 [2, 2, 8, 16, 512, 128], P(None, None, 'grp', None, 'seq'), parts along dimension 2, may hold values from -6 to 6
- prompt_ids: int32 [2, 8, 512], P(None, 'grp'), parts along dimension 1, may hold values from 0 to 32127, as said below
- timesteps: int32 [8], P('grp'), parts along dimension 0, may hold values from 0 to 999
- image_states: bfloat16 [8, 896, 1536], P('grp', 'seq'), parts along dimension 0, may hold values from -6 to 6
- frozen_out: bfloat16 [2048, 1536], P('seq'), may hold values from -0.125 to 0.125
- trainee_out: bfloat16 [4096, 1536], P(('grp', 'seq')), parts along dimension 0, may hold values from -0.125 to 0.125
- time_mod: bfloat16 [256, 3072], replicated, may hold values from -0.375 to 0.375
- final_head: bfloat16 [1536, 64], replicated, may hold values from -0.15625 to 0.15625
Outputs:
- weight_grad: float32 [4096, 1536], P(('grp', 'seq')), parts along dimension 0
There are 2 independent parts, one for each index of `grp`. A program takes and returns all parts, laid end to end along the dimension named above; an argument that names none is the same for every part. Nothing has to cross between parts.
Inputs may be any that keep to these rules, and one draw needn't show every extreme that they name: `prompt_ids`: zero marks padding; in each row of 512 ids the padding is a suffix and position 0 is never padding.
All inputs are finite; a program needn't handle non-finite values.
Results may differ from a plain program's by a relative error of at most 0.011.
Values may be sent and summed in bfloat16 or wider, within the bound.
No kernel may reach another device: no remote copies, remote signals or barrier semaphores. Data moves between devices by JAX's collectives and lax.ppermute only.
A program may use at most 128 MiB of HBM per device.

v0:
```python
import math
import jax
import jax.numpy as jnp
from jax import lax
from jax.sharding import PartitionSpec as P

SAMPLES = 4
HEADS = 16
HEAD_DIM = 128
WIDTH = 1536
TIME_DIM = 256


def image_block(queries, image_keys, image_values):
    factor = HEAD_DIM ** (-0.5)
    image_scores = jnp.dot(queries, image_keys.T, preferred_element_type=jnp.float32) * factor
    image_max = jnp.max(image_scores, axis=1, keepdims=True)
    image_exp = jnp.exp(image_scores - image_max)
    image_total = jnp.sum(image_exp, axis=1, keepdims=True)
    image_part = jnp.dot(
        image_exp.astype(jnp.bfloat16), image_values, preferred_element_type=jnp.float32
    )
    return (image_max, image_total, image_part)


def text_finish(queries, image_stats, text_keys, text_values, allowed_text):
    factor = HEAD_DIM ** (-0.5)
    image_max, image_total, image_part = image_stats
    text_scores = jnp.dot(queries, text_keys.T, preferred_element_type=jnp.float32) * factor
    text_scores = jnp.where(allowed_text[None, :], text_scores, -jnp.inf)
    pass_max = jnp.maximum(image_max, jnp.max(text_scores, axis=1, keepdims=True))
    ratio = jnp.exp(image_max - pass_max)
    text_exp = jnp.exp(text_scores - pass_max)
    text_part = jnp.dot(
        text_exp.astype(jnp.bfloat16), text_values, preferred_element_type=jnp.float32
    )
    numer = ratio * image_part + text_part
    denom = ratio * image_total + jnp.sum(text_exp, axis=1, keepdims=True)
    return (numer / denom).astype(jnp.bfloat16)


def head_out(branch, states, gate, scale, final_head):
    mixed = states.astype(jnp.float32) + gate[:, None, :] * branch
    normed = (
        mixed
        * lax.rsqrt(jnp.mean(mixed * mixed, axis=-1, keepdims=True) + 1e-06)
        * (1.0 + scale[:, None, :])
    )
    normed = normed.astype(jnp.bfloat16)
    return jnp.einsum("bic,cd->bid", normed, final_head, preferred_element_type=jnp.float32)


def shards(
    image_qkv,
    text_kv,
    prompt_ids,
    timesteps,
    image_states,
    frozen_out,
    trainee_out,
    time_mod,
    final_head,
):
    group_size = lax.axis_size("seq")
    position = lax.axis_index("seq")
    image_dev = image_qkv.shape[3]
    text_dev = text_kv.shape[4]
    item_count = SAMPLES * HEADS
    owned_count = item_count // group_size
    token_rows = SAMPLES * image_dev
    image_all = image_dev * group_size
    block_rows = image_dev * min(group_size, 8)
    block_count = image_all // block_rows
    image_local = image_qkv.transpose(0, 2, 1, 3, 4).reshape(3, item_count, image_dev, HEAD_DIM)
    text_local = text_kv.transpose(0, 1, 3, 2, 4, 5).reshape(4, item_count, text_dev, HEAD_DIM)
    image_heads, text_heads = (
        lax.all_to_all(image_local, "seq", split_axis=1, concat_axis=2, tiled=True),
        lax.all_to_all(text_local, "seq", split_axis=1, concat_axis=2, tiled=True),
    )
    owned_items = position * owned_count + jnp.arange(owned_count, dtype=jnp.int32)
    sample_of = owned_items % SAMPLES
    selector = (sample_of[:, None] == jnp.arange(SAMPLES, dtype=jnp.int32)[None, :]).astype(
        jnp.float32
    )
    live_all = (prompt_ids != 0).astype(jnp.float32)
    live_owned = jnp.einsum("jb,pbt->pjt", selector, live_all) > 0.5

    def query_blocks(item_index):
        return image_heads[0, item_index].reshape(block_count, block_rows, HEAD_DIM)

    def joint_item(item_index):
        image_keys = image_heads[1, item_index]
        image_values = image_heads[2, item_index]

        def per_block(queries):
            stats = image_block(queries, image_keys, image_values)
            concept = text_finish(
                queries,
                stats,
                text_heads[0, item_index],
                text_heads[1, item_index],
                live_owned[0, item_index],
            )
            null = text_finish(
                queries,
                stats,
                text_heads[2, item_index],
                text_heads[3, item_index],
                live_owned[1, item_index],
            )
            return jnp.stack([concept, null])

        blocks = lax.map(per_block, query_blocks(item_index))
        return blocks.transpose(1, 0, 2, 3).reshape(2, image_all, HEAD_DIM)

    both_passes = lax.map(joint_item, jnp.arange(owned_count, dtype=jnp.int32)).transpose(
        1, 0, 2, 3
    )
    returned = lax.all_to_all(both_passes, "seq", split_axis=2, concat_axis=1, tiled=True)
    attention = returned.reshape(2, HEADS, SAMPLES, image_dev, HEAD_DIM).transpose(0, 2, 3, 1, 4)
    attention = attention.reshape(2, token_rows, HEADS * HEAD_DIM)
    half_dim = TIME_DIM // 2
    freqs = jnp.exp(-math.log(10000.0) * jnp.arange(half_dim, dtype=jnp.float32) / half_dim)
    angles = timesteps.astype(jnp.float32)[:, None] * freqs[None, :]
    embedding = jnp.concatenate([jnp.cos(angles), jnp.sin(angles)], 1)
    modulation = jnp.dot(embedding, time_mod.astype(jnp.float32), precision=lax.Precision.HIGHEST)
    gate = modulation[:, :WIDTH]
    scale = modulation[:, WIDTH:]
    piece_frozen = lax.all_gather(frozen_out, "seq", axis=0, tiled=True)
    piece_trainee = lax.all_gather(trainee_out, "seq", axis=0, tiled=True)
    columns_c = attention[0]
    columns_n = attention[1]
    branch_c = jnp.dot(columns_c, piece_frozen, preferred_element_type=jnp.float32)
    branch_n = jnp.dot(columns_n, piece_frozen, preferred_element_type=jnp.float32)
    branch_s = jnp.dot(columns_c, piece_trainee, preferred_element_type=jnp.float32)
    branch_c = branch_c.reshape(SAMPLES, image_dev, WIDTH)
    branch_n = branch_n.reshape(SAMPLES, image_dev, WIDTH)
    branch_s = branch_s.reshape(SAMPLES, image_dev, WIDTH)
    velocity_c = head_out(branch_c, image_states, gate, scale, final_head)
    velocity_n = head_out(branch_n, image_states, gate, scale, final_head)
    target = velocity_n - (velocity_c - velocity_n)

    def student(branch):
        velocity_s = head_out(branch, image_states, gate, scale, final_head)
        return jnp.sum((velocity_s - target) ** 2) / SAMPLES

    loss_part, pull = jax.vjp(student, branch_s)
    (cotangent,) = pull(jnp.ones_like(loss_part))
    cotangent_samples = cotangent.astype(jnp.bfloat16)
    cotangent_rows = cotangent_samples.reshape(token_rows, WIDTH)
    columns = attention[0]
    return lax.psum_scatter(
        lax.dot_general(
            columns, cotangent_rows, (((0,), (0,)), ((), ())), preferred_element_type=jnp.float32
        ),
        "seq",
        scatter_dimension=0,
        tiled=True,
    )


def solution(mesh):
    return jax.shard_map(
        shards,
        mesh=mesh,
        in_specs=(
            P(None, "grp", None, "seq", None),
            P(None, None, "grp", None, "seq", None),
            P(None, "grp", None),
            P("grp"),
            P("grp", "seq", None),
            P("seq", None),
            P(("grp", "seq"), None),
            P(),
            P(),
        ),
        out_specs=P(("grp", "seq"), None),
        check_vma=False,
    )
```

profile of v0, /device:TPU:0, one launch (start us, length us, event | category | flops | bytes accessed | tf_op | source)
XLA Modules:
  0.0 544.9 jit_solution(13315047425198892459)
XLA Ops:
  7.3 2.2 copy.27
  11.4 7.4 %all-to-all-start.1 = ((bf16[4,64,32,128]{3,2,0,1:T(8,128)(2,1)}), bf16[4,64,32,128]{3,2,0,1:T(8,128)(2,1)}, u32[]{:S(2)}, u32[]{:S(2)}) async-start(bf16[4,64,32,128]{3,2,0,1:T(8,128)(2,1)} %copy.28), calls=%async_computation.1 | async-start | bytes 4194304 | tf_op jit(solution)/shard_map/all_to_all | solution.py:78
  18.9 2.4 copy.23
  23.3 49.5 %all-to-all-done.1 = bf16[4,64,32,128]{3,2,0,1:T(8,128)(2,1)} async-done(((bf16[4,64,32,128]{3,2,0,1:T(8,128)(2,1)}), bf16[4,64,32,128]{3,2,0,1:T(8,128)(2,1)}, u32[]{:S(2)}, u32[]{:S(2)}) %all-to-all-start.1) | async-done | bytes 2097184 | tf_op jit(solution)/shard_map/all_to_all | solution.py:78
  72.8 33.3 %all-to-all-start = ((bf16[3,64,56,128]{3,2,0,1:T(8,128)(2,1)}), bf16[3,64,56,128]{3,2,0,1:T(8,128)(2,1)}, u32[]{:S(2)}, u32[]{:S(2)}) async-start(bf16[3,64,56,128]{3,2,0,1:T(8,128)(2,1)} %copy.24), calls=%async_computation | async-start | bytes 5505024 | tf_op jit(solution)/shard_map/all_to_all | solution.py:77
  107.1 3.4 copy.30
  110.6 72.9 %all-to-all-done = bf16[3,64,56,128]{3,2,0,1:T(8,128)(2,1)} async-done(((bf16[3,64,56,128]{3,2,0,1:T(8,128)(2,1)}), bf16[3,64,56,128]{3,2,0,1:T(8,128)(2,1)}, u32[]{:S(2)}, u32[]{:S(2)}) %all-to-all-start) | async-done | bytes 2752544 | tf_op jit(solution)/shard_map/all_to_all | solution.py:77
  183.5 4.0 copy.26
  187.4 113.6 %while.23 = (s32[]{:T(128)}, bf16[4,2,896,128]{3,1,0,2:T(2,128)(2,1)}, s32[4]{0:T(128)S(1)}, bf16[3,4,896,128]{3,2,1,0:T(8,128)(2,1)}, pred[2,4,512]{2,1,0:T(4,1...) while((s32[]{:T(128)}, ...), condition=%wide.region_9.10_spmd, body=%wide.region_0.9_spmd.sunk | while | flops 447742848 | bytes 26686016 | solution.py:116
  193.9 19.6 %while.24 = (s32[]{:T(128)}, bf16[2,2,448,128]{3,2,1,0:T(8,128)(2,1)}, bf16[2,448,128]{2,1,0:T(8,128)(2,1)S(1)}, bf16[896,128]{1,0:T(8,128)(2,1)}, pred[1,1,512]...) while((s32[]{:T(128)}, ...), condition=%wide.region_8.8_spmd, body=%wide.region_1.7_spmd.sunk | while | flops 447742848 | bytes 22390328 | solution.py:113
  195.9 2.1 fusion.139
  222.3 19.6 %while.24 = (s32[]{:T(128)}, bf16[2,2,448,128]{3,2,1,0:T(8,128)(2,1)}, bf16[2,448,128]{2,1,0:T(8,128)(2,1)S(1)}, bf16[896,128]{1,0:T(8,128)(2,1)}, pred[1,1,512]...) while((s32[]{:T(128)}, ...), condition=%wide.region_8.8_spmd, body=%wide.region_1.7_spmd.sunk | while | flops 447742848 | bytes 22390328 | solution.py:113
  250.7 19.6 %while.24 = (s32[]{:T(128)}, bf16[2,2,448,128]{3,2,1,0:T(8,128)(2,1)}, bf16[2,448,128]{2,1,0:T(8,128)(2,1)S(1)}, bf16[896,128]{1,0:T(8,128)(2,1)}, pred[1,1,512]...) while((s32[]{:T(128)}, ...), condition=%wide.region_8.8_spmd, body=%wide.region_1.7_spmd.sunk | while | flops 447742848 | bytes 22390328 | solution.py:113
  279.1 19.6 %while.24 = (s32[]{:T(128)}, bf16[2,2,448,128]{3,2,1,0:T(8,128)(2,1)}, bf16[2,448,128]{2,1,0:T(8,128)(2,1)S(1)}, bf16[896,128]{1,0:T(8,128)(2,1)}, pred[1,1,512]...) while((s32[]{:T(128)}, ...), condition=%wide.region_8.8_spmd, body=%wide.region_1.7_spmd.sunk | while | flops 447742848 | bytes 22390328 | solution.py:113
  301.1 27.2 %all-to-all-start.2 = ((bf16[2,4,896,128]{3,0,1,2:T(2,128)(2,1)}), bf16[2,4,896,128]{3,0,1,2:T(2,128)(2,1)}, u32[]{:S(2)}, u32[]{:S(2)}) async-start(bf16[2,4,896,128]{3,0,1,2:T(2,128)(2,1)} %bitcast.168), calls=%async_computation.2 | async-start | bytes 3670016 | tf_op jit(solution)/shard_map/all_to_all | solution.py:119
  329.4 35.5 %all-to-all-done.2 = bf16[2,4,896,128]{3,0,1,2:T(2,128)(2,1)} async-done(((bf16[2,4,896,128]{3,0,1,2:T(2,128)(2,1)}), bf16[2,4,896,128]{3,0,1,2:T(2,128)(2,1)}, u32[]{:S(2)}, u32[]{:S(2)}) %all-to-all-start.2) | async-done | bytes 1835040 | tf_op jit(solution)/shard_map/all_to_all | solution.py:119
  364.9 2.7 copy.44
  370.1 2.2 dot_general.69
  372.4 4.9 multiply_reduce_fusion.4
  377.3 5.0 multiply_reduce_fusion.3
  382.7 2.8 multiply_reduce_fusion.2
  386.4 3.4 multiply_reduce_fusion.1
  391.6 6.4 %fusion.70 = f32[2048,1536]{1,0:T(8,128)} fusion(bf16[224,1536]{1,0:T(8,128)(2,1)S(1)} %bitcast.167, bf16[28,8,16,128]{3,2,1,0:T(8,128)(2,1)S(1)} %bitcast.164), kind=kOutput, calls=%fused_computation.90 | convolution fusion | flops 1409286144 | bytes 14188544 | tf_op jit(solution)/shard_map/dot_general | solution.py:153
  398.0 140.3 %reduce-scatter.2.cloned.1.call-done = f32[128,1536]{1,0:T(8,128)} async-done(((f32[2048,1536]{1,0:T(8,128)}), f32[128,1536]{1,0:T(8,128)}) %reduce-scatter.2.cloned.1.call-update) | async-done | bytes 786448 | tf_op jit(solution)/shard_map/reduce_scatter | solution.py:152
  (305 shorter events, 115.1 us)
Async XLA Ops:
  6.5 322.1 %copy-start = (bf16[256,3072]{1,0:T(8,128)(2,1)S(1)}, bf16[256,3072]{1,0:T(8,128)(2,1)}, u32[]{:S(2)}) copy-start(bf16[256,3072]{1,0:T(8,128)(2,1)} %param.20) | copy-start | bytes 4718596
  6.5 365.8 %all-gather.3.cloned.1.call-start = ((), (), s32[]{:S(2)}) async-start(), calls=%async_computation.4 | async-start | bytes 6684672 | tf_op jit(solution)/shard_map/all_gather | solution.py:130
  11.4 61.4 %all-to-all-start.1 = ((bf16[4,64,32,128]{3,2,0,1:T(8,128)(2,1)}), bf16[4,64,32,128]{3,2,0,1:T(8,128)(2,1)}, u32[]{:S(2)}, u32[]{:S(2)}) async-start(bf16[4,64,32,128]{3,2,0,1:T(8,128)(2,1)} %copy.28), calls=%async_computation.1 | async-start | bytes 4194304 | tf_op jit(solution)/shard_map/all_to_all | solution.py:78
  23.3 83.6 %copy-start.15 = (s32[2,4,512]{2,1,0:T(4,128)S(1)}, s32[2,4,512]{2,1,0:T(4,128)}, u32[]{:S(2)}) copy-start(s32[2,4,512]{2,1,0:T(4,128)} %param.15) | copy-start | bytes 49156
  72.8 110.7 %all-to-all-start = ((bf16[3,64,56,128]{3,2,0,1:T(8,128)(2,1)}), bf16[3,64,56,128]{3,2,0,1:T(8,128)(2,1)}, u32[]{:S(2)}, u32[]{:S(2)}) async-start(bf16[3,64,56,128]{3,2,0,1:T(8,128)(2,1)} %copy.24), calls=%async_computation | async-start | bytes 5505024 | tf_op jit(solution)/shard_map/all_to_all | solution.py:77
  106.1 271.1 %all-gather.5.cloned.1.call-start = ((), (), s32[]{:S(2)}) async-start(), calls=%async_computation.5 | async-start | bytes 6684672 | tf_op jit(solution)/shard_map/all_gather | solution.py:129
  187.4 2.5 copy-start.17
  187.4 6.4 %copy-start.11 = (pred[2,4,512]{2,1,0:T(4,128)(4,1)}, pred[2,4,512]{2,1,0:T(4,128)(4,1)S(1)}, u32[]{:S(2)}) copy-start(pred[2,4,512]{2,1,0:T(4,128)(4,1)S(1)} %get-tuple-element.467) | copy-start | bytes 12292 | tf_op jit(solution)/shard_map/while
  215.9 2.5 copy-start.17
  215.9 6.4 %copy-start.11 = (pred[2,4,512]{2,1,0:T(4,128)(4,1)}, pred[2,4,512]{2,1,0:T(4,128)(4,1)S(1)}, u32[]{:S(2)}) copy-start(pred[2,4,512]{2,1,0:T(4,128)(4,1)S(1)} %get-tuple-element.467) | copy-start | bytes 12292 | tf_op jit(solution)/shard_map/while
  241.9 2.4 copy-start.12
  241.9 2.4 copy-start.18
  244.3 2.5 copy-start.17
  244.3 6.4 %copy-start.11 = (pred[2,4,512]{2,1,0:T(4,128)(4,1)}, pred[2,4,512]{2,1,0:T(4,128)(4,1)S(1)}, u32[]{:S(2)}) copy-start(pred[2,4,512]{2,1,0:T(4,128)(4,1)S(1)} %get-tuple-element.467) | copy-start | bytes 12292 | tf_op jit(solution)/shard_map/while
  272.7 2.5 copy-start.17
  272.7 6.4 %copy-start.11 = (pred[2,4,512]{2,1,0:T(4,128)(4,1)}, pred[2,4,512]{2,1,0:T(4,128)(4,1)S(1)}, u32[]{:S(2)}) copy-start(pred[2,4,512]{2,1,0:T(4,128)(4,1)S(1)} %get-tuple-element.467) | copy-start | bytes 12292 | tf_op jit(solution)/shard_map/while
  301.1 27.4 %copy-start.16 = (s32[4]{0:T(128)S(1)}, s32[4]{0:T(128)}, u32[]{:S(2)}) copy-start(s32[4]{0:T(128)} %param.16) | copy-start | bytes 52
  301.1 63.8 %all-to-all-start.2 = ((bf16[2,4,896,128]{3,0,1,2:T(2,128)(2,1)}), bf16[2,4,896,128]{3,0,1,2:T(2,128)(2,1)}, u32[]{:S(2)}, u32[]{:S(2)}) async-start(bf16[2,4,896,128]{3,0,1,2:T(2,128)(2,1)} %bitcast.168), calls=%async_computation.2 | async-start | bytes 3670016 | tf_op jit(solution)/shard_map/all_to_all | solution.py:119
  328.2 210.1 %reduce-scatter.2.cloned.1.call-start = ((), (), s32[]{:S(2)}) async-start(), calls=%async_computation.6 | async-start | bytes 13369344 | tf_op jit(solution)/shard_map/reduce_scatter | solution.py:152
  368.8 3.6 copy-start.5
  377.3 5.1 copy-start.10
  377.3 5.3 copy-start.13
  377.3 5.4 copy-start.14
  382.7 2.9 copy-start.9
  (55 other events, 66.2 us)
Sparse Core Ops, SparseCore 0:
  9.6 98.0 all-gather.2
  110.0 94.7 all-gather.4
  398.2 140.1 reduce-scatter.1
where the time goes:
time: 547 us; the launch traced here: 545 us
  waiting for transfers between devices  300 us (55%)
  matrix products  71 us (13%)
  starting transfers between devices  68.2 us (12%)
  local copies, waits for them, and re-layouts  63.1 us (12%)
  other arithmetic  20.9 us (4%)
  between operations  13.3 us (2%)
  loops' own time  8.68 us (2%)
    reduce_scatter x1, waiting for transfers between devices, shards(): lax.psum_scatter(lax.dot_general(columns, cotangent_rows, (((0,), (0,)),...  140 us
    all_to_all x1, waiting for transfers between devices, shards(): lax.all_to_all(image_local, 'seq', split_axis=1, concat_axis=2, tiled=True)  72.9 us
    all_to_all x1, waiting for transfers between devices, shards(): lax.all_to_all(text_local, 'seq', split_axis=1, concat_axis=2, tiled=True)  49.5 us
    all_to_all x1, waiting for transfers between devices, shards(): lax.all_to_all(both_passes, 'seq', split_axis=2, concat_axis=1, tiled=True)  35.5 us
    all_to_all x1, starting transfers between devices, shards(): lax.all_to_all(image_local, 'seq', split_axis=1, concat_axis=2, tiled=True)  33.3 us
    all_to_all x1, starting transfers between devices, shards(): lax.all_to_all(both_passes, 'seq', split_axis=2, concat_axis=1, tiled=True)  27.2 us
    dot_general x16, matrix products, text_finish(): jnp.dot(queries, text_keys.T, preferred_element_type=jnp.float32) * factor  25.9 us
    while x128, local copies, waits for them, and re-layouts  12.1 us
  transfers between devices with their start and end apart: 6, of which 4 were waited for; matrix products, arithmetic and copies ran while one was open for 22% of the time, Pallas kernels for 0%

commit v1 on v0

--- a/solution.py
+++ b/solution.py
@@ -116,7 +116,12 @@
     both_passes = lax.map(joint_item, jnp.arange(owned_count, dtype=jnp.int32)).transpose(
         1, 0, 2, 3
     )
-    returned = lax.all_to_all(both_passes, "seq", split_axis=2, concat_axis=1, tiled=True)
+    returned = jnp.concatenate(
+        lax.all_to_all(
+            jnp.stack(jnp.split(both_passes, lax.axis_size("seq"), axis=2)), "seq", 0, 0
+        ),
+        axis=1,
+    )
     attention = returned.reshape(2, HEADS, SAMPLES, image_dev, HEAD_DIM).transpose(0, 2, 3, 1, 4)
     attention = attention.reshape(2, token_rows, HEADS * HEAD_DIM)
     half_dim = TIME_DIM // 2

time: 547 us -> 555 us (1.015)
  local copies, waits for them, and re-layouts: 63.1 us -> 74.5 us
    unnamed x20 -> x39, local copies, waits for them, and re-layouts: 5 us -> 22.1 us
    dot_general x8, matrix products: 3.86 us -> 11.5 us  [image_block(): jnp.dot(image_exp.astype(jnp.bfloat16), image_values, preferred_element_t...]
    while x128 -> x112, local copies, waits for them, and re-layouts: 12.1 us -> 8.65 us
  transfers between devices with their start and end apart: 6 -> 6, of which waited for: 4 -> 4; matrix products, arithmetic and copies ran while one was open for 22% -> 24% of each run, Pallas kernels for 0% -> 0%
where the time goes in v1:
time: 555 us; the launch traced here: 553 us
  waiting for transfers between devices  299 us (54%)
  local copies, waits for them, and re-layouts  74.5 us (13%)
  matrix products  73.2 us (13%)
  starting transfers between devices  68.1 us (12%)
  other arithmetic  16.3 us (3%)
  between operations  13.3 us (2%)
  loops' own time  8.48 us (2%)
    reduce_scatter x1, waiting for transfers between devices, shards(): lax.psum_scatter(lax.dot_general(columns, cotangent_rows, (((0,), (0,)),...  140 us
    all_to_all x1, waiting for transfers between devices, shards(): lax.all_to_all(image_local, 'seq', split_axis=1, concat_axis=2, tiled=True)  72.9 us
    all_to_all x1, waiting for transfers between devices, shards(): lax.all_to_all(text_local, 'seq', split_axis=1, concat_axis=2, tiled=True)  49.5 us
    all_to_all x1, waiting for transfers between devices, shards(): lax.all_to_all(jnp.stack(jnp.split(both_passes, lax.axis_size('seq'), axi...  35.4 us
    all_to_all x1, starting transfers between devices, shards(): lax.all_to_all(image_local, 'seq', split_axis=1, concat_axis=2, tiled=True)  33.3 us
    all_to_all x1, starting transfers between devices, shards(): lax.all_to_all(jnp.stack(jnp.split(both_passes, lax.axis_size('seq'), axi...  27.1 us
    unnamed x39, local copies, waits for them, and re-layouts  22.1 us
    dot_general x16, matrix products, text_finish(): jnp.dot(queries, text_keys.T, preferred_element_type=jnp.float32) * factor  20.6 us
  transfers between devices with their start and end apart: 6, of which 4 were waited for; matrix products, arithmetic and copies ran while one was open for 24% of the time, Pallas kernels for 0%

profile of v1, /device:TPU:0, one launch (start us, length us, event | category | flops | bytes accessed | tf_op | source)
XLA Modules:
  0.0 553.3 jit_solution(9149514357397811513)
XLA Ops:
  7.3 2.2 copy.32
  11.4 7.4 %all-to-all-start.1 = ((bf16[4,64,32,128]{3,2,0,1:T(8,128)(2,1)}), bf16[4,64,32,128]{3,2,0,1:T(8,128)(2,1)}, u32[]{:S(2)}, u32[]{:S(2)}) async-start(bf16[4,64,32,128]{3,2,0,1:T(8,128)(2,1)} %copy.33), calls=%async_computation.1 | async-start | bytes 4194304 | tf_op jit(solution)/shard_map/all_to_all | solution.py:78
  18.9 2.4 copy.28
  21.3 2.0 copy.29
  23.3 49.5 %all-to-all-done.1 = bf16[4,64,32,128]{3,2,0,1:T(8,128)(2,1)} async-done(((bf16[4,64,32,128]{3,2,0,1:T(8,128)(2,1)}), bf16[4,64,32,128]{3,2,0,1:T(8,128)(2,1)}, u32[]{:S(2)}, u32[]{:S(2)}) %all-to-all-start.1) | async-done | bytes 2097184 | tf_op jit(solution)/shard_map/all_to_all | solution.py:78
  72.8 33.3 %all-to-all-start = ((bf16[3,64,56,128]{3,2,0,1:T(8,128)(2,1)}), bf16[3,64,56,128]{3,2,0,1:T(8,128)(2,1)}, u32[]{:S(2)}, u32[]{:S(2)}) async-start(bf16[3,64,56,128]{3,2,0,1:T(8,128)(2,1)} %copy.29), calls=%async_computation | async-start | bytes 5505024 | tf_op jit(solution)/shard_map/all_to_all | solution.py:77
  107.2 3.4 copy.35
  110.6 72.9 %all-to-all-done = bf16[3,64,56,128]{3,2,0,1:T(8,128)(2,1)} async-done(((bf16[3,64,56,128]{3,2,0,1:T(8,128)(2,1)}), bf16[3,64,56,128]{3,2,0,1:T(8,128)(2,1)}, u32[]{:S(2)}, u32[]{:S(2)}) %all-to-all-start) | async-done | bytes 2752544 | tf_op jit(solution)/shard_map/all_to_all | solution.py:77
  183.5 4.0 copy.31
  187.5 105.8 %while.23 = (s32[]{:T(128)}, bf16[4,2,896,128]{3,2,1,0:T(8,128)(2,1)}, s32[4]{0:T(128)S(1)}, bf16[3,4,896,128]{3,2,1,0:T(8,128)(2,1)}, pred[2,4,512]{2,1,0:T(4,1...) while((s32[]{:T(128)}, ...), condition=%wide.region_9.10_spmd, body=%wide.region_0.9_spmd.sunk | while | flops 447742848 | bytes 25767992 | solution.py:116
  190.0 2.0 dynamic-slice_bitcast_fusion.3
  193.9 18.2 %while.24 = (s32[]{:T(128)}, bf16[2,2,448,128]{3,2,1,0:T(8,128)(2,1)}, bf16[2,448,128]{2,1,0:T(8,128)(2,1)S(1)}, bf16[896,128]{1,0:T(8,128)(2,1)}, pred[1,1,512]...) while((s32[]{:T(128)}, ...), condition=%wide.region_8.8_spmd, body=%wide.region_1.7_spmd.sunk | while | flops 447742848 | bytes 21472804 | solution.py:113
  220.4 18.1 %while.24 = (s32[]{:T(128)}, bf16[2,2,448,128]{3,2,1,0:T(8,128)(2,1)}, bf16[2,448,128]{2,1,0:T(8,128)(2,1)S(1)}, bf16[896,128]{1,0:T(8,128)(2,1)}, pred[1,1,512]...) while((s32[]{:T(128)}, ...), condition=%wide.region_8.8_spmd, body=%wide.region_1.7_spmd.sunk | while | flops 447742848 | bytes 21472804 | solution.py:113
  246.8 18.1 %while.24 = (s32[]{:T(128)}, bf16[2,2,448,128]{3,2,1,0:T(8,128)(2,1)}, bf16[2,448,128]{2,1,0:T(8,128)(2,1)S(1)}, bf16[896,128]{1,0:T(8,128)(2,1)}, pred[1,1,512]...) while((s32[]{:T(128)}, ...), condition=%wide.region_8.8_spmd, body=%wide.region_1.7_spmd.sunk | while | flops 447742848 | bytes 21472804 | solution.py:113
  273.2 18.1 %while.24 = (s32[]{:T(128)}, bf16[2,2,448,128]{3,2,1,0:T(8,128)(2,1)}, bf16[2,448,128]{2,1,0:T(8,128)(2,1)S(1)}, bf16[896,128]{1,0:T(8,128)(2,1)}, pred[1,1,512]...) while((s32[]{:T(128)}, ...), condition=%wide.region_8.8_spmd, body=%wide.region_1.7_spmd.sunk | while | flops 447742848 | bytes 21472804 | solution.py:113
  311.1 27.1 %all-to-all-start.2 = ((bf16[16,2,4,56,128]{4,3,1,2,0:T(8,128)(2,1)}), bf16[16,2,4,56,128]{4,3,1,2,0:T(8,128)(2,1)S(1)}, u32[]{:S(2)}, u32[]{:S(2)}) async-start(bf16[16,2,4,56,128]{4,3,1,2,0:T(8,128)(2,1)} %fusion.87), calls=%async_computation.2 | async-start | bytes 3670016 | tf_op jit(solution)/shard_map/all_to_all | solution.py:120
  339.3 35.4 %all-to-all-done.2 = bf16[16,2,4,56,128]{4,3,1,2,0:T(8,128)(2,1)S(1)} async-done(((bf16[16,2,4,56,128]{4,3,1,2,0:T(8,128)(2,1)}), bf16[16,2,4,56,128]{4,3,1,2,0:T(8,128)(2,1)S(1)}, u32[]{:S(2)}, u32[]{:S(2)}) %all-to-all-start.2) | async-done | bytes 1835040 | tf_op jit(solution)/shard_map/all_to_all | solution.py:120
  378.8 2.2 dot_general.69
  381.0 4.9 multiply_reduce_fusion.4
  386.0 5.0 multiply_reduce_fusion.3
  391.4 2.8 multiply_reduce_fusion.2
  395.0 3.4 multiply_reduce_fusion.1
  400.2 6.4 %fusion.70 = f32[2048,1536]{1,0:T(8,128)} fusion(bf16[224,1536]{1,0:T(8,128)(2,1)S(1)} %bitcast.228, bf16[28,8,16,128]{3,2,1,0:T(8,128)(2,1)S(1)} %bitcast.225), kind=kOutput, calls=%fused_computation.89 | convolution fusion | flops 1409286144 | bytes 14188544 | tf_op jit(solution)/shard_map/dot_general | solution.py:158
  406.6 140.1 %reduce-scatter.2.cloned.1.call-done = f32[128,1536]{1,0:T(8,128)} async-done(((f32[2048,1536]{1,0:T(8,128)}), f32[128,1536]{1,0:T(8,128)}) %reduce-scatter.2.cloned.1.call-update) | async-done | bytes 786448 | tf_op jit(solution)/shard_map/reduce_scatter | solution.py:157
  (310 shorter events, 124.9 us)
Async XLA Ops:
  6.5 332.0 %copy-start = (bf16[256,3072]{1,0:T(8,128)(2,1)S(1)}, bf16[256,3072]{1,0:T(8,128)(2,1)}, u32[]{:S(2)}) copy-start(bf16[256,3072]{1,0:T(8,128)(2,1)} %param.20) | copy-start | bytes 4718596
  6.5 374.5 %all-gather.3.cloned.1.call-start = ((), (), s32[]{:S(2)}) async-start(), calls=%async_computation.4 | async-start | bytes 6684672 | tf_op jit(solution)/shard_map/all_gather | solution.py:135
  11.4 61.4 %all-to-all-start.1 = ((bf16[4,64,32,128]{3,2,0,1:T(8,128)(2,1)}), bf16[4,64,32,128]{3,2,0,1:T(8,128)(2,1)}, u32[]{:S(2)}, u32[]{:S(2)}) async-start(bf16[4,64,32,128]{3,2,0,1:T(8,128)(2,1)} %copy.33), calls=%async_computation.1 | async-start | bytes 4194304 | tf_op jit(solution)/shard_map/all_to_all | solution.py:78
  23.3 83.6 %copy-start.16 = (s32[2,4,512]{2,1,0:T(4,128)S(1)}, s32[2,4,512]{2,1,0:T(4,128)}, u32[]{:S(2)}) copy-start(s32[2,4,512]{2,1,0:T(4,128)} %param.15) | copy-start | bytes 49156
  72.8 110.7 %all-to-all-start = ((bf16[3,64,56,128]{3,2,0,1:T(8,128)(2,1)}), bf16[3,64,56,128]{3,2,0,1:T(8,128)(2,1)}, u32[]{:S(2)}, u32[]{:S(2)}) async-start(bf16[3,64,56,128]{3,2,0,1:T(8,128)(2,1)} %copy.29), calls=%async_computation | async-start | bytes 5505024 | tf_op jit(solution)/shard_map/all_to_all | solution.py:77
  106.2 279.8 %all-gather.5.cloned.1.call-start = ((), (), s32[]{:S(2)}) async-start(), calls=%async_computation.5 | async-start | bytes 6684672 | tf_op jit(solution)/shard_map/all_gather | solution.py:134
  187.5 4.5 copy-start.12
  197.1 2.9 copy-start.1
  206.2 2.8 copy-start.1
  213.9 4.5 copy-start.12
  223.6 2.8 copy-start.1
  232.7 2.8 copy-start.1
  240.4 4.5 copy-start.12
  259.1 2.8 copy-start.1
  266.8 4.5 copy-start.12
  276.5 2.8 copy-start.1
  285.5 2.8 copy-start.1
  293.3 12.6 %copy-start.10 = (bf16[4,2,896,128]{3,2,1,0:T(8,128)(2,1)S(1)}, bf16[4,2,896,128]{3,2,1,0:T(8,128)(2,1)}, u32[]{:S(2)}) copy-start(bf16[4,2,896,128]{3,2,1,0:T(8,128)(2,1)} %get-tuple-element.153) | copy-start | bytes 5505028
  311.1 27.3 %copy-start.17 = (s32[4]{0:T(128)S(1)}, s32[4]{0:T(128)}, u32[]{:S(2)}) copy-start(s32[4]{0:T(128)} %param.16) | copy-start | bytes 52
  311.1 63.6 %all-to-all-start.2 = ((bf16[16,2,4,56,128]{4,3,1,2,0:T(8,128)(2,1)}), bf16[16,2,4,56,128]{4,3,1,2,0:T(8,128)(2,1)S(1)}, u32[]{:S(2)}, u32[]{:S(2)}) async-start(bf16[16,2,4,56,128]{4,3,1,2,0:T(8,128)(2,1)} %fusion.87), calls=%async_computation.2 | async-start | bytes 3670016 | tf_op jit(solution)/shard_map/all_to_all | solution.py:120
  338.1 208.6 %reduce-scatter.2.cloned.1.call-start = ((), (), s32[]{:S(2)}) async-start(), calls=%async_computation.6 | async-start | bytes 13369344 | tf_op jit(solution)/shard_map/reduce_scatter | solution.py:157
  385.9 5.1 copy-start.11
  385.9 5.3 copy-start.14
  386.0 5.4 copy-start.15
  (49 other events, 65.9 us)
Sparse Core Ops, SparseCore 0:
  9.6 98.0 all-gather.2
  110.0 94.8 all-gather.4
  406.8 139.9 reduce-scatter.1
